TPU v7x, 128 devices: a whole 4x4x4 slice. The times are simulated.
128 devices in a mesh: brick: 64 (over z_lo, x, y, core), vec: 2 (over z_hi).
Axes of the slice: x: 4, y: 4, z: 4 (z_hi: 2, z_lo: 2; z = z_hi * 2 + z_lo), core: 2. Of those that a mesh axis runs over, the one named last changes fastest.
Arguments:
- levels: int32 [12, 2048, 16, 128], P(None, 'brick'), may hold values from 0 to 255
- start_block: int32 [16, 2048, 16, 128], P('vec', 'brick'), may hold values from -8 to 8
Outputs:
- alpha_blocks: float32 [1, 16, 16], replicated
- beta_blocks: float32 [1, 16, 16], replicated
- basis: float32 [16, 2048, 16, 128], P('vec', 'brick')
All inputs are finite; a program needn't handle non-finite values.
Results may differ from a plain program's by a relative error of at most 0.00026.
Values sent between devices are 32-bit elements; how exact they have to be, the bound alone decides.
No kernel may reach another device: no remote copies, remote signals or barrier semaphores. Data moves between devices by JAX's collectives and lax.ppermute only.
A program may use at most 128 MiB of HBM per device.

v0:
```python
import math
import jax
import jax.numpy as jnp
from jax import lax
from jax.sharding import PartitionSpec as P

offsets_cube = (1, 3, 9, 27)
deepest = 27
highest = lax.Precision.HIGHEST


def passed_along(value, axis, by):
    size = lax.axis_size(axis)
    pairs = [(i, i + by) for i in range(size) if 0 <= i + by < size]
    return lax.ppermute(value, axis, pairs)


def forward_take(field_in, offset, axis_dim):
    length_dim = field_in.shape[axis_dim]
    widths = [(0, 0)] * field_in.ndim
    widths[axis_dim] = (0, offset)
    return lax.slice_in_dim(jnp.pad(field_in, widths), offset, offset + length_dim, axis=axis_dim)


def backward_put(field_in, offset, axis_dim):
    length_dim = field_in.shape[axis_dim]
    widths = [(0, 0)] * field_in.ndim
    widths[axis_dim] = (offset, 0)
    return lax.slice_in_dim(jnp.pad(field_in, widths), 0, length_dim, axis=axis_dim)


def local_planes(field_in, weights, result):
    for axis_dim in (2, 3):
        for position, offset in enumerate(offsets_cube):
            channel = weights[4 * (axis_dim - 1) + position]
            result = (
                result
                + channel * forward_take(field_in, offset, axis_dim)
                + backward_put(channel * field_in, offset, axis_dim)
            )
    return result


def apply_carried(field_in, weights):
    row_count = field_in.shape[1]
    upper_rows = passed_along(field_in[:, :deepest], "brick", -1)
    extended = jnp.concatenate([field_in, upper_rows], axis=1)
    result = jnp.zeros_like(field_in)
    spilled = jnp.zeros_like(upper_rows)
    for position, offset in enumerate(offsets_cube):
        channel = weights[position]
        result = result + channel * extended[:, offset : offset + row_count]
        shifted_rows = jnp.pad(
            channel * field_in, ((0, 0), (offset, deepest - offset), (0, 0), (0, 0))
        )
        result = result + shifted_rows[:, :row_count]
        spilled = spilled + shifted_rows[:, row_count:]
    result = local_planes(field_in, weights, result)
    arrived = passed_along(spilled, "brick", 1)
    return result + jnp.pad(arrived, ((0, 0), (0, row_count - deepest), (0, 0), (0, 0)))


def inner_of(left_rows, right_rows):
    return jnp.einsum("in,jn->ij", left_rows, right_rows, precision=highest)


def body(levels, start_block):
    weights = (levels.astype(jnp.float32) + 0.5) / 256.0

    def affinity_apply(field_in):
        return apply_carried(field_in, weights)

    unit_field = jnp.ones((1,) + levels.shape[1:], jnp.float32)
    degree = affinity_apply(unit_field)[0] + 1.0
    inv_root = lax.rsqrt(degree)

    def half_step(block_in):
        return 0.5 * (block_in + inv_root * affinity_apply(inv_root * block_in))

    own_cols = start_block.shape[0]
    grid_shape = start_block.shape
    voxel_total = lax.axis_size("brick") * grid_shape[1] * grid_shape[2] * grid_shape[3]

    def to_work(block_in):
        flat_block = block_in.reshape(own_cols, -1)
        work_rows = lax.all_gather(flat_block, "vec", axis=0, tiled=True)
        return work_rows

    def from_work(work_rows):
        own_rows = lax.dynamic_slice_in_dim(
            work_rows, lax.axis_index("vec") * own_cols, own_cols, 0
        )
        return own_rows.reshape(grid_shape)

    def total_one(partial_sum):
        summed = lax.psum(partial_sum, "brick")
        return summed

    start_work = to_work(start_block.astype(jnp.float32))
    lower_factor = jnp.linalg.cholesky(total_one(inner_of(start_work, start_work)))
    current = lax.linalg.triangular_solve(lower_factor, start_work, left_side=True, lower=True)
    basis_now = from_work(current)
    image_block = to_work(half_step(half_step(basis_now)))
    coeffs = total_one(inner_of(image_block, current))
    residual = image_block - jnp.einsum("ij,jn->in", coeffs, current, precision=highest)
    gram_matrix = total_one(inner_of(residual, residual))
    lower_factor = jnp.linalg.cholesky(gram_matrix)
    following = lax.linalg.triangular_solve(lower_factor, residual, left_side=True, lower=True)
    alpha_list = [coeffs]
    beta_list = [lower_factor]
    basis_now = from_work(following)
    basis = basis_now * math.sqrt(voxel_total)
    return (jnp.stack(alpha_list), jnp.stack(beta_list), basis)


def solution(mesh):
    return jax.shard_map(
        body,
        mesh=mesh,
        in_specs=(P(None, "brick", None, None), P("vec", "brick", None, None)),
        out_specs=(P(), P(), P("vec", "brick", None, None)),
        check_vma=False,
    )
```

profile of v0, /device:TPU:1, one launch (start us, length us, event | category | flops | bytes accessed | tf_op | source)
XLA Modules:
  0.0 726.9 jit_solution(13446341821634345445)
XLA Ops:
  7.2 1.7 convert_element_type.111
  9.0 2.5 copy.14
  12.3 3.3 collective-permute-start
  15.6 2.3 add_multiply_fusion
  20.1 3.2 collective-permute-start.1
  26.5 2.7 broadcast_multiply_fusion.24
  29.2 48.8 %all-gather.3.cloned.1.call-done = f32[16,65536]{1,0:T(8,128)} async-done(((f32[8,65536]{1,0:T(8,128)}), f32[16,65536]{1,0:T(8,128)}) %all-gather.3.cloned.1.call-update) | async-done | bytes 4194320 | tf_op jit(solution)/shard_map/all_gather | solution.py:86
  78.0 9.0 %fusion.127 = f32[16,16]{0,1:T(8,128)S(1)} fusion(f32[16,65536]{1,0:T(8,128)} %all-gather.3.cloned.1.call-done), kind=kOutput, calls=%fused_computation.264 | convolution fusion | flops 201326592 | bytes 4195328 | tf_op jit(solution)/shard_map/in,jn->ij/dot_general | solution.py:64
  87.0 140.6 %psum.21 = f32[16,16]{0,1:T(8,128)S(1)} all-reduce(f32[16,16]{0,1:T(8,128)S(1)} %fusion.127), channel_id=1, replica_groups=mesh['brick'=64,'vec'=2] {'brick'}, use_global_device_ids=true, to_apply=%region_0.1 | all-reduce | flops 256 | bytes 2048 | tf_op jit(solution)/shard_map/psum | solution.py:96
  231.7 5.4 fusion.122
  237.3 1.8 copy-done.1
  239.1 2.1 broadcast_multiply_fusion.14
  241.4 4.7 collective-permute-start.2
  246.1 5.1 broadcast_multiply_fusion.12
  252.6 2.1 collective-permute-start.3
  254.7 10.7 %collective-permute-done.2 = f32[8,27,16,128]{3,0,2,1:T(8,128)S(1)} collective-permute-done((f32[8,27,16,128]{3,0,2,1:T(8,128)S(1)}, f32[8,27,16,128]{3,0,2,1:T(8,128)S(1)}, u32[]{:S(2)}, u32[]{:S(2)}) %collective-permute-start.2) | collective-permute-done | bytes 1769504 | tf_op jit(solution)/shard_map/ppermute | solution.py:15
  265.3 8.6 %collective-permute-done.3 = f32[8,27,16,128]{3,0,2,1:T(8,128)S(1)} collective-permute-done((f32[8,27,16,128]{3,0,2,1:T(8,128)S(1)}, f32[8,27,16,128]{3,0,2,1:T(8,128)S(1)}, u32[]{:S(2)}, u32[]{:S(2)}) %collective-permute-start.3) | collective-permute-done | bytes 1769504 | tf_op jit(solution)/shard_map/ppermute | solution.py:15
  275.2 12.9 %broadcast_multiply_fusion.13 = (f32[8,32,16,128]{3,0,2,1:T(8,128)}, f32[8,32,16,128]{3,0,2,1:T(8,128)S(1)}, f32[8,32,16,128]{3,0,2,1:T(8,128)}) fusion(f32[32,16,128]{2,1,0:T(8,128)} %get-tuple-element.20, f32[32,16,128]{2,1,0:T(8,128)} %get-tuple-element.11, f32[8,32,16,128]{3,0,2,1:T(8,128)} %bitcast.67, f32[8,27,16,128]{3,0,2,1:T(8,128)} %copy-done.32, ...), kind=kLoop, calls=%fused_computation.155 | loop fusion | flops 22020096 | bytes 40763392 | tf_op jit(solution)/shard_map/mul | solution.py:39
  289.6 5.1 broadcast_multiply_fusion.11
  294.7 1.9 collective-permute-start.4
  296.8 4.5 collective-permute-start.5
  301.3 17.9 %collective-permute-done.4 = f32[8,27,16,128]{3,0,2,1:T(8,128)S(1)} collective-permute-done((f32[8,27,16,128]{3,0,2,1:T(8,128)S(1)}, f32[8,27,16,128]{3,0,2,1:T(8,128)S(1)}, u32[]{:S(2)}, u32[]{:S(2)}) %collective-permute-start.4) | collective-permute-done | bytes 1769504 | tf_op jit(solution)/shard_map/ppermute | solution.py:15
  322.0 11.3 %add_multiply_fusion.1 = f32[8,32,16,128]{3,0,2,1:T(8,128)} fusion(f32[8,32,16,128]{3,0,2,1:T(8,128)} %get-tuple-element.10, f32[8,27,16,128]{3,0,2,1:T(8,128)} %copy-done.30, f32[8,32,16,128]{3,0,2,1:T(8,128)} %get-tuple-element.40, f32[8,32,16,128]{3,0,2,1:T(8,128)S(1)} %get-tuple-element.9, f32[8,32,16,128]{3,0,2,1:T(8,128)} %get-tuple-element.47, ...), kind=kLoop, calls=%fused_computation.134 | loop fusion | flops 22020096 | bytes 36306944 | tf_op jit(solution)/shard_map/mul | solution.py:78
  333.3 65.7 %all-gather.5.cloned.1.call-done = f32[16,65536]{1,0:T(8,128)} async-done(((f32[8,65536]{1,0:T(8,128)}), f32[16,65536]{1,0:T(8,128)}) %all-gather.5.cloned.1.call-update) | async-done | bytes 4194320 | tf_op jit(solution)/shard_map/all_gather | solution.py:86
  399.0 8.7 %fusion.128 = f32[16,16]{1,0:T(8,128)S(1)} fusion(f32[16,65536]{1,0:T(8,128)} %all-gather.5.cloned.1.call-done, f32[16,65536]{1,0:T(8,128)} %copy-done.1), kind=kOutput, calls=%fused_computation.265 | convolution fusion | flops 201326592 | bytes 8389632 | tf_op jit(solution)/shard_map/in,jn->ij/dot_general | solution.py:64
  407.7 140.9 %psum.22 = f32[16,16]{1,0:T(8,128)S(1)} all-reduce(f32[16,16]{1,0:T(8,128)S(1)} %fusion.128), channel_id=1, replica_groups=mesh['brick'=64,'vec'=2] {'brick'}, use_global_device_ids=true, to_apply=%region_3.6 | all-reduce | flops 256 | bytes 2048 | tf_op jit(solution)/shard_map/psum | solution.py:96
  548.6 7.1 convolution_subtract_fusion
  555.7 1.9 copy-done
  557.7 5.6 fusion.129
  563.3 144.8 %psum.23 = f32[16,16]{0,1:T(8,128)S(1)} all-reduce(f32[16,16]{0,1:T(8,128)S(1)} %fusion.129), channel_id=1, replica_groups=mesh['brick'=64,'vec'=2] {'brick'}, use_global_device_ids=true, to_apply=%region_4.7 | all-reduce | flops 256 | bytes 2048 | tf_op jit(solution)/shard_map/psum | solution.py:96
  712.8 5.4 fusion.119
  718.4 1.7 copy.9
  (100 shorter events, 22.3 us)
Async XLA Ops:
  7.2 70.8 %all-gather.3.cloned.1.call-start = ((), (), s32[]{:S(2)}) async-start(), calls=%async_computation | async-start | bytes 6291456 | tf_op jit(solution)/shard_map/all_gather | solution.py:86
  11.5 387.5 %all-gather.5.cloned.1.call-start = ((), (), s32[]{:S(2)}) async-start(), calls=%async_computation.1 | async-start | bytes 6291456 | tf_op jit(solution)/shard_map/all_gather | solution.py:86
  12.3 12.7 %collective-permute-start = (f32[1,27,16,128]{3,2,1,0:T(8,128)}, f32[1,27,16,128]{3,2,1,0:T(8,128)}, u32[]{:S(2)}, u32[]{:S(2)}) collective-permute-start(f32[1,27,16,128]{3,2,1,0:T(8,128)} %slice.322), channel_id=1, source_target_pairs={{2,0},{4,2},{6,4},{8,6},{10,8},{12,10},{14,12},{16,14},{18,16},{20... | collective-permute-start | bytes 663560 | tf_op jit(solution)/shard_map/ppermute | solution.py:15
  18.7 1.4 copy-start.25
  18.7 4.6 copy-start.27
  20.1 6.4 collective-permute-start.1
  23.3 3.2 copy-start.24
  23.3 3.2 copy-start.26
  23.3 3.2 copy-start.28
  23.3 3.2 copy-start.33
  237.1 2.0 copy-start.1
  237.1 2.0 copy-start.21
  237.1 1.9 copy-start.22
  239.1 2.1 copy-start.2
  241.2 4.9 copy-start.5
  241.2 4.9 copy-start.6
  241.2 4.9 copy-start.7
  241.2 4.9 copy-start.9
  241.2 4.9 copy-start.11
  241.2 4.9 copy-start.13
  241.2 4.9 copy-start.15
  241.2 4.9 copy-start.17
  241.2 4.9 copy-start.19
  241.4 24.0 %collective-permute-start.2 = (f32[8,27,16,128]{3,0,2,1:T(8,128)S(1)}, f32[8,27,16,128]{3,0,2,1:T(8,128)S(1)}, u32[]{:S(2)}, u32[]{:S(2)}) collective-permute-start(f32[8,27,16,128]{3,0,2,1:T(8,128)S(1)} %slice.428), channel_id=1, source_target_pairs={{2,0},{4,2},{6,4},{8,6},{10,8},{12,10},{14,12},{16,14},{18,16},{20... | collective-permute-start | bytes 5308424 | tf_op jit(solution)/shard_map/ppermute | solution.py:15
  252.6 21.4 %collective-permute-start.3 = (f32[8,27,16,128]{3,0,2,1:T(8,128)S(1)}, f32[8,27,16,128]{3,0,2,1:T(8,128)S(1)}, u32[]{:S(2)}, u32[]{:S(2)}) collective-permute-start(f32[8,27,16,128]{3,0,2,1:T(8,128)S(1)} %fusion.76), channel_id=1, source_target_pairs={{0,2},{2,4},{4,6},{6,8},{8,10},{10,12},{12,14},{14,16},{16,18},{18... | collective-permute-start | bytes 5308424 | tf_op jit(solution)/shard_map/ppermute | solution.py:15
  265.3 8.6 %copy-start.31 = (f32[8,27,16,128]{3,0,2,1:T(8,128)}, f32[8,27,16,128]{3,0,2,1:T(8,128)S(1)}, u32[]{:S(2)}) copy-start(f32[8,27,16,128]{3,0,2,1:T(8,128)S(1)} %collective-permute-done.2) | copy-start | bytes 5308420
  294.7 24.6 %collective-permute-start.4 = (f32[8,27,16,128]{3,0,2,1:T(8,128)S(1)}, f32[8,27,16,128]{3,0,2,1:T(8,128)S(1)}, u32[]{:S(2)}, u32[]{:S(2)}) collective-permute-start(f32[8,27,16,128]{3,0,2,1:T(8,128)S(1)} %slice.436), channel_id=1, source_target_pairs={{2,0},{4,2},{6,4},{8,6},{10,8},{12,10},{14,12},{16,14},{18,16},{20... | collective-permute-start | bytes 5308424 | tf_op jit(solution)/shard_map/ppermute | solution.py:15
  296.6 25.4 %copy-start.4 = (f32[8,32,16,128]{3,0,2,1:T(8,128)S(1)}, f32[8,32,16,128]{3,0,2,1:T(8,128)}, u32[]{:S(2)}) copy-start(f32[8,32,16,128]{3,0,2,1:T(8,128)} %get-tuple-element.8) | copy-start | bytes 6291460
  296.8 24.0 %collective-permute-start.5 = (f32[8,27,16,128]{3,0,2,1:T(8,128)S(1)}, f32[8,27,16,128]{3,0,2,1:T(8,128)S(1)}, u32[]{:S(2)}, u32[]{:S(2)}) collective-permute-start(f32[8,27,16,128]{3,0,2,1:T(8,128)S(1)} %fusion.79), channel_id=1, source_target_pairs={{0,2},{2,4},{4,6},{6,8},{8,10},{10,12},{12,14},{14,16},{16,18},{18... | collective-permute-start | bytes 5308424 | tf_op jit(solution)/shard_map/ppermute | solution.py:15
  319.2 1.5 copy-start.29
  548.6 7.1 copy-start.34
  555.7 2.0 copy-start
  (11 other events, 12.7 us)
Sparse Core Ops, SparseCore 0:
  11.6 66.3 all-gather.2
  333.4 65.5 all-gather.4
where the time goes:
time: 727 us
  blocking collectives  426 us (59%)
  waiting for transfers between devices  155 us (21%)
  other arithmetic  54.6 us (8%)
  matrix products  41.2 us (6%)
  starting transfers between devices  19.7 us (3%)
  local copies, waits for them, and re-layouts  15.7 us (2%)
  between operations  14.6 us (2%)
    psum x3, blocking collectives, total_one(): summed = lax.psum(partial_sum, 'brick')  426 us
    all_gather x2, waiting for transfers between devices, to_work(): work_rows = lax.all_gather(flat_block, 'vec', axis=0, tiled=True)  115 us
    ppermute x6, waiting for transfers between devices, passed_along(): return lax.ppermute(value, axis, pairs)  40.2 us
    mul x4, other arithmetic, local_planes(): channel * field_in  25.2 us
    dot_general x3, matrix products, inner_of(): return jnp.einsum('in,jn->ij', left_rows, right_rows, precision=highest)  23.3 us
    ppermute x6, starting transfers between devices, passed_along(): return lax.ppermute(value, axis, pairs)  19.7 us
  transfers between devices with their start and end apart: 8, of which 7 were waited for; matrix products, arithmetic and copies ran while one was open for 2% of the time, Pallas kernels for 0%

commit v1 on v0

--- a/solution.py
+++ b/solution.py
@@ -3,6 +3,7 @@
 import jax.numpy as jnp
 from jax import lax
 from jax.sharding import PartitionSpec as P
+from jax.lax import all_to_all, axis_size
 
 offsets_cube = (1, 3, 9, 27)
 deepest = 27
@@ -83,7 +84,15 @@
 
     def to_work(block_in):
         flat_block = block_in.reshape(own_cols, -1)
-        work_rows = lax.all_gather(flat_block, "vec", axis=0, tiled=True)
+        work_rows = jnp.concatenate(
+            all_to_all(
+                jnp.stack([flat_block for _ in range(axis_size("vec"))], axis=0),
+                axis_name="vec",
+                split_axis=0,
+                concat_axis=0,
+            ),
+            0,
+        )
         return work_rows
 
     def from_work(work_rows):

time: 727 us -> 696 us (0.957)
  waiting for transfers between devices: 155 us -> 75 us
  blocking collectives: 426 us -> 469 us
  between operations: 14.6 us -> 1.16 us
  starting transfers between devices: 19.7 us -> 27.7 us
  other arithmetic: 54.6 us -> 61.9 us
    all_gather x2 -> x0, waiting for transfers between devices: 115 us -> none  [to_work(): work_rows = lax.all_gather(flat_block, 'vec', axis=0, tiled=True)]
    all_to_all x0 -> x1, blocking collectives: none -> 36 us  [to_work(): all_to_all(jnp.stack([flat_block for _ in range(axis_size('vec'))], axis=...]
    all_to_all x0 -> x1, waiting for transfers between devices: none -> 34.9 us  [to_work(): all_to_all(jnp.stack([flat_block for _ in range(axis_size('vec'))], axis=...]
  transfers between devices with their start and end apart: 8 -> 7, of which waited for: 7 -> 6; matrix products, arithmetic and copies ran while one was open for 2% -> 2% of each run, Pallas kernels for 0% -> 0%
where the time goes in v1:
time: 696 us; the launch traced here: 690 us
  blocking collectives  469 us (67%)
  waiting for transfers between devices  75 us (11%)
  other arithmetic  61.9 us (9%)
  matrix products  39.4 us (6%)
  starting transfers between devices  27.7 us (4%)
  local copies, waits for them, and re-layouts  15.2 us (2%)
    psum x3, blocking collectives, total_one(): summed = lax.psum(partial_sum, 'brick')  433 us
    ppermute x6, waiting for transfers between devices, passed_along(): return lax.ppermute(value, axis, pairs)  40.2 us
    all_to_all x1, blocking collectives, to_work(): all_to_all(jnp.stack([flat_block for _ in range(axis_size('vec'))], axis=...  36 us
    all_to_all x1, waiting for transfers between devices, to_work(): all_to_all(jnp.stack([flat_block for _ in range(axis_size('vec'))], axis=...  34.9 us
    mul x4, other arithmetic, local_planes(): channel * field_in  25.8 us
    ppermute x6, starting transfers between devices, passed_along(): return lax.ppermute(value, axis, pairs)  22 us
    dot_general x3, matrix products, inner_of(): return jnp.einsum('in,jn->ij', left_rows, right_rows, precision=highest)  21.5 us
    mul x2, other arithmetic, half_step(): return 0.5 * (block_in + inv_root * affinity_apply(inv_root * block_in))  14.4 us
  transfers between devices with their start and end apart: 7, of which 6 were waited for; matrix products, arithmetic and copies ran while one was open for 2% of the time, Pallas kernels for 0%

profile of v1, /device:TPU:1, one launch (start us, length us, event | category | flops | bytes accessed | tf_op | source)
XLA Modules:
  0.0 689.7 jit_solution(351898135808151558)
XLA Ops:
  0.6 3.1 convert_element_type.111
  3.7 2.0 stack_reshape.8
  5.7 2.3 pad_maximum_fusion
  8.0 5.7 all-to-all-start
  14.4 3.2 collective-permute-start
  17.6 2.3 add_multiply_fusion
  22.1 3.2 collective-permute-start.1
  28.6 2.6 broadcast_multiply_fusion.24
  31.1 34.9 %all-to-all-done = f32[2,8,65536]{2,1,0:T(8,128)} async-done(((f32[2,8,65536]{2,1,0:T(8,128)}), f32[2,8,65536]{2,1,0:T(8,128)}, u32[]{:S(2)}, u32[]{:S(2)}) %all-to-all-start) | async-done | bytes 4194336 | tf_op jit(solution)/shard_map/all_to_all | solution.py:88
  66.0 9.0 %fusion.4 = f32[16,16]{0,1:T(8,128)S(1)} fusion(f32[2,8,65536]{2,1,0:T(8,128)} %all-to-all-done), kind=kOutput, calls=%fused_computation.31 | convolution fusion | flops 201326592 | bytes 4195328 | tf_op jit(solution)/shard_map/in,jn->ij/dot_general | solution.py:65
  75.0 141.2 %psum.21 = f32[16,16]{0,1:T(8,128)S(1)} all-reduce(f32[16,16]{0,1:T(8,128)S(1)} %fusion.4), channel_id=1, replica_groups=mesh['brick'=64,'vec'=2] {'brick'}, use_global_device_ids=true, to_apply=%region_0.1 | all-reduce | flops 256 | bytes 2048 | tf_op jit(solution)/shard_map/psum | solution.py:105
  220.2 5.4 fusion.2
  227.1 2.0 broadcast_multiply_fusion.14
  229.3 7.2 %collective-permute-start.2 = (f32[8,27,16,128]{3,0,2,1:T(8,128)S(1)}, f32[8,27,16,128]{3,0,2,1:T(8,128)}, u32[]{:S(2)}, u32[]{:S(2)}) collective-permute-start(f32[8,27,16,128]{3,0,2,1:T(8,128)S(1)} %slice.428), channel_id=1, source_target_pairs={{2,0},{4,2},{6,4},{8,6},{10,8},{12,10},{14,12},{16,14},{18,16},{20... | collective-permute-start | bytes 5308424 | tf_op jit(solution)/shard_map/ppermute | solution.py:16
  236.6 5.0 broadcast_multiply_fusion.12
  243.6 2.1 collective-permute-start.3
  245.7 7.6 %collective-permute-done.2 = f32[8,27,16,128]{3,0,2,1:T(8,128)} collective-permute-done((f32[8,27,16,128]{3,0,2,1:T(8,128)S(1)}, f32[8,27,16,128]{3,0,2,1:T(8,128)}, u32[]{:S(2)}, u32[]{:S(2)}) %collective-permute-start.2) | collective-permute-done | bytes 1769504 | tf_op jit(solution)/shard_map/ppermute | solution.py:16
  253.3 11.6 %collective-permute-done.3 = f32[8,27,16,128]{3,0,2,1:T(8,128)S(1)} collective-permute-done((f32[8,27,16,128]{3,0,2,1:T(8,128)S(1)}, f32[8,27,16,128]{3,0,2,1:T(8,128)S(1)}, u32[]{:S(2)}, u32[]{:S(2)}) %collective-permute-start.3) | collective-permute-done | bytes 1769504 | tf_op jit(solution)/shard_map/ppermute | solution.py:16
  266.2 13.7 %broadcast_multiply_fusion.13 = (f32[8,32,16,128]{3,0,2,1:T(8,128)}, f32[8,32,16,128]{3,0,2,1:T(8,128)S(1)}, f32[8,32,16,128]{3,0,2,1:T(8,128)}) fusion(f32[32,16,128]{2,1,0:T(8,128)} %get-tuple-element.20, f32[32,16,128]{2,1,0:T(8,128)} %get-tuple-element.11, f32[8,32,16,128]{3,0,2,1:T(8,128)} %bitcast.69, f32[8,27,16,128]{3,0,2,1:T(8,128)} %copy-done.33, ...), kind=kLoop, calls=%fused_computation.162 | loop fusion | flops 22020096 | bytes 40763392 | tf_op jit(solution)/shard_map/mul | solution.py:40
  281.4 5.1 broadcast_multiply_fusion.11
  288.6 4.4 collective-permute-start.5
  293.0 18.1 %collective-permute-done.4 = f32[8,27,16,128]{3,0,2,1:T(8,128)S(1)} collective-permute-done((f32[8,27,16,128]{3,0,2,1:T(8,128)S(1)}, f32[8,27,16,128]{3,0,2,1:T(8,128)S(1)}, u32[]{:S(2)}, u32[]{:S(2)}) %collective-permute-start.4) | collective-permute-done | bytes 1769504 | tf_op jit(solution)/shard_map/ppermute | solution.py:16
  313.7 11.8 %add_multiply_fusion.1 = f32[8,32,16,128]{3,0,2,1:T(8,128)} fusion(f32[8,32,16,128]{3,0,2,1:T(8,128)} %get-tuple-element.10, f32[8,27,16,128]{3,0,2,1:T(8,128)} %copy-done.32, f32[8,32,16,128]{3,0,2,1:T(8,128)} %get-tuple-element.40, f32[8,32,16,128]{3,0,2,1:T(8,128)S(1)} %get-tuple-element.9, f32[8,32,16,128]{3,0,2,1:T(8,128)} %get-tuple-element.47, ...), kind=kLoop, calls=%fused_computation.141 | loop fusion | flops 22020096 | bytes 36306944 | tf_op jit(solution)/shard_map/mul | solution.py:79
  325.5 2.5 pad_maximum_fusion.1
  328.0 36.0 %all_to_all.10 = f32[2,8,65536]{2,1,0:T(8,128)} all-to-all(f32[2,8,65536]{2,1,0:T(8,128)S(1)} %pad_maximum_fusion.1), channel_id=1, replica_groups=mesh['brick'=64,'vec'=2] {'vec'}, dimensions={0} | all-to-all | bytes 8388608 | tf_op jit(solution)/shard_map/all_to_all | solution.py:88
  364.0 6.9 fusion
  370.9 151.7 %psum.22 = f32[16,16]{1,0:T(8,128)S(1)} all-reduce(f32[16,16]{1,0:T(8,128)S(1)} %fusion), channel_id=1, replica_groups=mesh['brick'=64,'vec'=2] {'brick'}, use_global_device_ids=true, to_apply=%region_3.6 | all-reduce | flops 256 | bytes 2048 | tf_op jit(solution)/shard_map/psum | solution.py:105
  522.6 7.1 %convolution_subtract_fusion = f32[16,65536]{1,0:T(8,128)S(1)} fusion(f32[16,16]{1,0:T(8,128)S(1)} %psum.22, f32[16,65536]{1,0:T(8,128)} %copy-done.1, f32[2,8,65536]{2,1,0:T(8,128)} %all_to_all.10), kind=kOutput, calls=%fused_computation | convolution fusion | flops 202375168 | bytes 12583936 | tf_op jit(solution)/shard_map/ij,jn->in/dot_general | solution.py:114
  529.7 2.0 copy-done
  531.7 5.6 fusion.132
  537.3 140.5 %psum.23 = f32[16,16]{0,1:T(8,128)S(1)} all-reduce(f32[16,16]{0,1:T(8,128)S(1)} %fusion.132), channel_id=1, replica_groups=mesh['brick'=64,'vec'=2] {'brick'}, use_global_device_ids=true, to_apply=%region_4.7 | all-reduce | flops 256 | bytes 2048 | tf_op jit(solution)/shard_map/psum | solution.py:105
  682.5 5.4 fusion.125
  (101 shorter events, 27.6 us)
Async XLA Ops:
  8.0 58.0 %all-to-all-start = ((f32[2,8,65536]{2,1,0:T(8,128)}), f32[2,8,65536]{2,1,0:T(8,128)}, u32[]{:S(2)}, u32[]{:S(2)}) async-start(f32[2,8,65536]{2,1,0:T(8,128)} %pad_maximum_fusion), calls=%async_computation | async-start | bytes 8388608 | tf_op jit(solution)/shard_map/all_to_all | solution.py:88
  14.4 12.7 %collective-permute-start = (f32[1,27,16,128]{3,2,1,0:T(8,128)}, f32[1,27,16,128]{3,2,1,0:T(8,128)}, u32[]{:S(2)}, u32[]{:S(2)}) collective-permute-start(f32[1,27,16,128]{3,2,1,0:T(8,128)} %slice.322), channel_id=1, source_target_pairs={{2,0},{4,2},{6,4},{8,6},{10,8},{12,10},{14,12},{16,14},{18,16},{20... | collective-permute-start | bytes 663560 | tf_op jit(solution)/shard_map/ppermute | solution.py:16
  20.7 1.4 copy-start.27
  20.7 4.6 copy-start.29
  22.1 6.4 collective-permute-start.1
  25.4 3.2 copy-start.26
  25.4 3.2 copy-start.28
  25.4 3.2 copy-start.30
  25.4 3.2 copy-start.34
  225.7 138.3 %copy-start.1 = (f32[16,65536]{1,0:T(8,128)}, f32[16,65536]{1,0:T(8,128)S(1)}, u32[]{:S(2)}) copy-start(f32[16,65536]{1,0:T(8,128)S(1)} %fusion.2) | copy-start | bytes 12582916
  225.7 1.4 copy-start.24
  225.8 3.2 copy-start.4
  229.1 7.4 %copy-start.7 = (f32[32,16,128]{2,1,0:T(8,128)S(1)}, f32[32,16,128]{2,1,0:T(8,128)}, u32[]{:S(2)}) copy-start(f32[32,16,128]{2,1,0:T(8,128)} %get-tuple-element.16) | copy-start | bytes 786436
  229.1 7.4 %copy-start.8 = (f32[32,16,128]{2,1,0:T(8,128)S(1)}, f32[32,16,128]{2,1,0:T(8,128)}, u32[]{:S(2)}) copy-start(f32[32,16,128]{2,1,0:T(8,128)} %get-tuple-element.17) | copy-start | bytes 786436
  229.1 7.4 %copy-start.9 = (f32[32,16,128]{2,1,0:T(8,128)S(1)}, f32[32,16,128]{2,1,0:T(8,128)}, u32[]{:S(2)}) copy-start(f32[32,16,128]{2,1,0:T(8,128)} %get-tuple-element.18) | copy-start | bytes 786436
  229.1 7.4 %copy-start.11 = (f32[32,16,128]{2,1,0:T(8,128)S(1)}, f32[32,16,128]{2,1,0:T(8,128)}, u32[]{:S(2)}) copy-start(f32[32,16,128]{2,1,0:T(8,128)} %get-tuple-element.19) | copy-start | bytes 786436
  229.1 7.4 %copy-start.13 = (f32[32,16,128]{2,1,0:T(8,128)S(1)}, f32[32,16,128]{2,1,0:T(8,128)}, u32[]{:S(2)}) copy-start(f32[32,16,128]{2,1,0:T(8,128)} %get-tuple-element.21) | copy-start | bytes 786436
  229.1 7.4 %copy-start.15 = (f32[32,16,128]{2,1,0:T(8,128)S(1)}, f32[32,16,128]{2,1,0:T(8,128)}, u32[]{:S(2)}) copy-start(f32[32,16,128]{2,1,0:T(8,128)} %get-tuple-element.22) | copy-start | bytes 786436
  229.1 7.4 %copy-start.17 = (f32[32,16,128]{2,1,0:T(8,128)S(1)}, f32[32,16,128]{2,1,0:T(8,128)}, u32[]{:S(2)}) copy-start(f32[32,16,128]{2,1,0:T(8,128)} %get-tuple-element.23) | copy-start | bytes 786436
  229.1 7.4 %copy-start.19 = (f32[32,16,128]{2,1,0:T(8,128)S(1)}, f32[32,16,128]{2,1,0:T(8,128)}, u32[]{:S(2)}) copy-start(f32[32,16,128]{2,1,0:T(8,128)} %get-tuple-element.24) | copy-start | bytes 786436
  229.1 7.4 %copy-start.21 = (f32[32,16,128]{2,1,0:T(8,128)S(1)}, f32[32,16,128]{2,1,0:T(8,128)}, u32[]{:S(2)}) copy-start(f32[32,16,128]{2,1,0:T(8,128)} %get-tuple-element.25) | copy-start | bytes 786436
  229.3 24.1 %collective-permute-start.2 = (f32[8,27,16,128]{3,0,2,1:T(8,128)S(1)}, f32[8,27,16,128]{3,0,2,1:T(8,128)}, u32[]{:S(2)}, u32[]{:S(2)}) collective-permute-start(f32[8,27,16,128]{3,0,2,1:T(8,128)S(1)} %slice.428), channel_id=1, source_target_pairs={{2,0},{4,2},{6,4},{8,6},{10,8},{12,10},{14,12},{16,14},{18,16},{20... | collective-permute-start | bytes 5308424 | tf_op jit(solution)/shard_map/ppermute | solution.py:16
  241.6 2.1 copy-start.6
  241.6 23.4 %copy-start.2 = (f32[8,32,16,128]{3,0,2,1:T(8,128)}, f32[8,32,16,128]{3,0,2,1:T(8,128)S(1)}, u32[]{:S(2)}) copy-start(f32[8,32,16,128]{3,0,2,1:T(8,128)S(1)} %get-tuple-element.55) | copy-start | bytes 6291460
  243.6 21.4 %collective-permute-start.3 = (f32[8,27,16,128]{3,0,2,1:T(8,128)S(1)}, f32[8,27,16,128]{3,0,2,1:T(8,128)S(1)}, u32[]{:S(2)}, u32[]{:S(2)}) collective-permute-start(f32[8,27,16,128]{3,0,2,1:T(8,128)S(1)} %fusion.82), channel_id=1, source_target_pairs={{0,2},{2,4},{4,6},{6,8},{8,10},{10,12},{12,14},{14,16},{16,18},{18... | collective-permute-start | bytes 5308424 | tf_op jit(solution)/shard_map/ppermute | solution.py:16
  280.0 1.4 copy-start.22
  286.5 2.1 copy-start.5
  286.5 24.6 %collective-permute-start.4 = (f32[8,27,16,128]{3,0,2,1:T(8,128)S(1)}, f32[8,27,16,128]{3,0,2,1:T(8,128)S(1)}, u32[]{:S(2)}, u32[]{:S(2)}) collective-permute-start(f32[8,27,16,128]{3,0,2,1:T(8,128)S(1)} %slice.436), channel_id=1, source_target_pairs={{2,0},{4,2},{6,4},{8,6},{10,8},{12,10},{14,12},{16,14},{18,16},{20... | collective-permute-start | bytes 5308424 | tf_op jit(solution)/shard_map/ppermute | solution.py:16
  288.6 23.8 %collective-permute-start.5 = (f32[8,27,16,128]{3,0,2,1:T(8,128)S(1)}, f32[8,27,16,128]{3,0,2,1:T(8,128)S(1)}, u32[]{:S(2)}, u32[]{:S(2)}) collective-permute-start(f32[8,27,16,128]{3,0,2,1:T(8,128)S(1)} %fusion.85), channel_id=1, source_target_pairs={{0,2},{2,4},{4,6},{6,8},{8,10},{10,12},{12,14},{14,16},{16,18},{18... | collective-permute-start | bytes 5308424 | tf_op jit(solution)/shard_map/ppermute | solution.py:16
  311.1 1.4 copy-start.31
  522.5 7.1 %copy-start.35 = (f32[16,16]{1,0:T(8,128)}, f32[16,16]{1,0:T(8,128)S(1)}, u32[]{:S(2)}) copy-start(f32[16,16]{1,0:T(8,128)S(1)} %psum.22) | copy-start | bytes 3076
  529.7 2.0 copy-start
  (11 other events, 12.5 us)
